TPU v7x, 512 devices: a whole 4x4x16 slice. The times are simulated.
512 devices in a mesh: grp: 16 (over z), feat: 32 (over y, x, core).
Axes of the slice: x: 4, y: 4, z: 16, core: 2. Of those that a mesh axis runs over, the one named last changes fastest.
Arguments:
- starting_latent_vectors: float32 [2048, 384], P(('grp', 'feat')), may hold values from -6 to 6
- run_driver_case: int32 [2048], P(('grp', 'feat')), may hold values from 0 to 7
- pair_table: int32 [2, 73920], P(None, 'feat'), may hold values from 0 to 383, as said below
- quadratic: bfloat16 [73920, 384], P('feat'), may hold values from -0.0234375 to 0.0234375
- linear: bfloat16 [384, 384], P('feat'), may hold values from -0.3125 to 0.3125
- forcing: float32 [8, 384], replicated, may hold values from -6 to 6
- basis: bfloat16 [2, 172032, 384], P(None, ('grp', 'feat')), may hold values from -0.3125 to 0.3125
- mean_fields: float32 [2, 172032], P(None, ('grp', 'feat')), may hold values from 1.5 to 3
Outputs:
- specific_weight_array: bfloat16 [172032, 2048], P(('grp', 'feat'))
- dimensionless_heat_measure: bfloat16 [172032, 2048], P(('grp', 'feat'))
Inputs may be any that keep to these rules, and one draw needn't show every extreme that they name: `pair_table`: every pair i <= j of state indices appears in exactly one column, with i in row 0 and j in row 1; columns are in a drawn order.
All inputs are finite; a program needn't handle non-finite values.
Results may differ from a plain program's by a relative error of at most 0.0065.
Values may be sent and summed in bfloat16 or wider, within the bound.
A program may use at most 64 MiB of HBM per device.

v0:
```python
import jax
import jax.numpy as jnp
from jax import lax
from jax.sharding import PartitionSpec as P

STEPS = 2


time_step = 0.25
min_volume = 0.25


def drift_terms(latent_vectors, first_index, second_index, linear, quadratic, feat_index):
    rounded = latent_vectors.astype(jnp.bfloat16)
    width = linear.shape[0]
    own_columns = lax.dynamic_slice_in_dim(rounded, feat_index * width, width, 1)
    features = (
        jnp.take(latent_vectors, first_index, axis=1)
        * jnp.take(latent_vectors, second_index, axis=1)
    ).astype(jnp.bfloat16)
    terms = jnp.dot(own_columns, linear, preferred_element_type=jnp.float32)
    return terms + jnp.dot(features, quadratic, preferred_element_type=jnp.float32)


def forcing_of(conditions, forcing):
    numbers = jnp.arange(forcing.shape[0], dtype=jnp.int32)
    onehot = (conditions[:, None] == numbers[None, :]).astype(jnp.float32)
    return jnp.dot(onehot, forcing, precision=lax.Precision.HIGHEST)


def lift_back_solution(ensemble_members, basis, mean_fields):
    cells = basis.shape[1]
    flat_basis = basis.reshape(2 * cells, basis.shape[2])
    flat_fields = lax.dot_general(
        flat_basis, ensemble_members, (((1,), (1,)), ((), ())), preferred_element_type=jnp.float32
    )
    fields = flat_fields.reshape(2, cells, ensemble_members.shape[0]) + mean_fields[:, :, None]
    volume = jnp.maximum(fields[0], min_volume)
    return jnp.stack([1.0 / volume, fields[1] * volume]).astype(jnp.bfloat16)


def per_device(
    starting_latent_vectors,
    run_driver_case,
    pair_table,
    quadratic,
    linear,
    forcing,
    basis,
    mean_fields,
):
    feat_index = lax.axis_index("feat")
    first_index = pair_table[0]
    second_index = pair_table[1]
    owned = starting_latent_vectors.shape[0]
    latent_vectors = starting_latent_vectors
    current = lax.all_gather(starting_latent_vectors, "feat", axis=0, tiled=True)
    own_forcing = forcing_of(run_driver_case, forcing)
    for step in range(STEPS):
        if step > 0:
            current = lax.all_gather(latent_vectors, "feat", axis=0, tiled=True)

        def block_quadratic_terms(row_start, row_count, source=current):
            return drift_terms(source, first_index, second_index, linear, quadratic, feat_index)

        summed = lax.psum_scatter(
            block_quadratic_terms(jnp.int32(0), owned * lax.axis_size("feat")),
            "feat",
            scatter_dimension=0,
            tiled=True,
        )
        latent_vectors = latent_vectors + time_step * (summed + own_forcing)
    outputs = lift_back_solution(
        lax.all_gather(latent_vectors.astype(jnp.bfloat16), ("grp", "feat"), axis=0, tiled=True),
        basis,
        mean_fields,
    )
    return (outputs[0], outputs[1])


def solution(mesh):
    return jax.shard_map(
        per_device,
        mesh=mesh,
        in_specs=(
            P(("grp", "feat"), None),
            P(("grp", "feat")),
            P(None, "feat"),
            P("feat", None),
            P("feat", None),
            P(),
            P(None, ("grp", "feat"), None),
            P(None, ("grp", "feat")),
        ),
        out_specs=(P(("grp", "feat"), None), P(("grp", "feat"), None)),
        check_vma=False,
    )
```

profile of v0, /device:TPU:1, one launch (start us, length us, event | category | flops | bytes accessed | tf_op | source)
XLA Modules:
  0.0 562.8 jit_solution(5031611944948704960)
XLA Ops:
  7.2 0.0 copy-start
  7.2 0.0 all-reduce.5.cloned.1.call-start
  7.2 0.9 slice_reduce_fusion.1
  8.2 29.1 %all-gather = f32[32,4,384]{2,1,0:T(4,128)S(1)} all-gather(f32[1,4,384]{2,1,0:T(4,128)} %bitcast.39), channel_id=1, replica_groups=mesh['grp'=16,'feat'=32] {'feat'}, dimensions={0}, use_global_device_ids=true | all-gather | bytes 202752 | tf_op jit(solution)/shard_map/all_gather | solution.py:57
  37.3 0.1 reshape.56
  37.4 0.1 copy.20
  37.5 4.2 gather_fusion.1
  41.7 0.0 copy-start.2
  41.7 5.6 gather_fusion
  47.3 0.0 copy-done.2
  47.3 0.2 fusion.13
  47.5 0.0 copy-done
  47.5 0.0 copy-start.4
  47.6 0.0 copy-start.5
  47.6 0.0 copy-start.1
  47.6 3.3 convolution_add_fusion.1
  50.8 0.0 all-reduce.5.cloned.1.call-update
  50.9 0.0 all-reduce.7.cloned.1.call-start
  50.9 0.0 copy-done.4
  50.9 0.0 copy-done.5
  50.9 0.2 fusion.21
  51.1 1.3 dynamic-slice
  53.0 128.0 %all-reduce.5.cloned.1.call-done = f32[128,384]{1,0:T(8,128)} async-done(((f32[128,384]{1,0:T(8,128)}), f32[128,384]{1,0:T(8,128)}) %all-reduce.5.cloned.1.call-update) | async-done | bytes 196624
  181.1 0.0 copy-done.1
  181.1 0.7 fusion.25
  181.8 24.6 %all-gather.1 = f32[32,4,384]{2,1,0:T(4,128)S(1)} all-gather(f32[1,4,384]{2,1,0:T(4,128)S(1)} %fusion.25), channel_id=1, replica_groups=mesh['grp'=16,'feat'=32] {'feat'}, dimensions={0}, use_global_device_ids=true | all-gather | bytes 202752 | tf_op jit(solution)/shard_map/all_gather | solution.py:61
  206.4 0.1 reshape.58
  206.4 0.2 fusion.14
  206.7 0.1 copy.22
  206.8 4.2 gather_fusion.3
  211.0 5.6 gather_fusion.2
  216.6 3.2 convolution_add_fusion
  219.8 0.0 all-reduce.7.cloned.1.call-update
  219.9 0.0 all-gather.5.cloned.1.call-start
  219.9 129.1 %all-reduce.7.cloned.1.call-done = f32[128,384]{1,0:T(8,128)} async-done(((f32[128,384]{1,0:T(8,128)}), f32[128,384]{1,0:T(8,128)}) %all-reduce.7.cloned.1.call-update) | async-done | bytes 196624
  349.0 1.3 fusion.20
  350.3 0.0 all-gather.5.cloned.1.call-update
  350.4 197.8 %all-gather.5.cloned.1.call-done = bf16[512,4,384]{2,1,0:T(4,128)(2,1)} async-done(((bf16[1,4,384]{2,1,0:T(4,128)(2,1)}), bf16[512,4,384]{2,1,0:T(4,128)(2,1)}) %all-gather.5.cloned.1.call-update) | async-done | bytes 1572880 | tf_op jit(solution)/shard_map/all_gather | solution.py:74
  548.1 2.7 reshape.60
  550.9 0.0 copy-start.3
  550.9 2.7 fusion.28
  553.6 0.0 copy-done.3
  553.6 0.4 broadcast_add_fusion
  554.0 2.3 fusion.1
  (4 shorter events, 0.0 us)
Async XLA Ops:
  7.2 40.4 %copy-start = (bf16[2310,384]{1,0:T(8,128)(2,1)S(1)}, bf16[2310,384]{1,0:T(8,128)(2,1)}, u32[]{:S(2)}) copy-start(bf16[2310,384]{1,0:T(8,128)(2,1)} %param.13) | copy-start | bytes 5322244
  7.2 173.9 %all-reduce.5.cloned.1.call-start = ((), (), s32[]{:S(2)}) async-start(), calls=%async_computation.1 | async-start | bytes 393216
  41.7 5.6 copy-start.2
  47.5 3.4 copy-start.4
  47.6 3.4 copy-start.5
  47.6 133.5 %copy-start.1 = (f32[4,384]{1,0:T(4,128)S(1)}, f32[4,384]{1,0:T(4,128)}, u32[]{:S(2)}) copy-start(f32[4,384]{1,0:T(4,128)} %param.10) | copy-start | bytes 18436
  50.9 298.2 %all-reduce.7.cloned.1.call-start = ((), (), s32[]{:S(2)}) async-start(), calls=%async_computation.2 | async-start | bytes 393216
  219.9 328.3 %all-gather.5.cloned.1.call-start = ((), (), s32[]{:S(2)}) async-start(), calls=%async_computation | async-start | bytes 1575936 | tf_op jit(solution)/shard_map/all_gather | solution.py:74
  550.9 2.7 copy-start.3
Sparse Core Ops, SparseCore 0:
  51.0 130.0 all-reduce.4
  220.0 129.0 all-reduce.6
  354.0 194.0 all-gather.4
where the time goes:
time: 563 us
  waiting for transfers between devices  455 us (81%)
  blocking collectives  53.7 us (10%)
  local copies, waits for them, and re-layouts  24.9 us (4%)
  between operations  14.6 us (3%)
  matrix products  9.81 us (2%)
    unnamed x5, waiting for transfers between devices  257 us
    all_gather x1, waiting for transfers between devices, per_device(): lax.all_gather(latent_vectors.astype(jnp.bfloat16), ('grp', 'feat'), axis...  198 us
    all_gather x1, blocking collectives, per_device(): lax.all_gather(starting_latent_vectors, 'feat', axis=0, tiled=True)  29.1 us
    all_gather x1, blocking collectives, per_device(): current = lax.all_gather(latent_vectors, 'feat', axis=0, tiled=True)  24.6 us
  transfers between devices with their start and end apart: 3, of which 3 were waited for; matrix products, arithmetic and copies ran while one was open for 0% of the time, Pallas kernels for 0%

commit v1 on v0

v1 whole, which is shorter than its diff:
```python
import functools

import jax
import jax.numpy as jnp
from jax import lax
from jax.experimental import pallas as pl
from jax.experimental.pallas import tpu as pltpu
from jax.sharding import PartitionSpec as P

STEPS = 2
time_step = 0.25
min_volume = 0.25
MESH = pl.DeviceIdType.MESH
TILE = 256
LINEAR_AT = 16


def wait_bytes(ref, count, sem):
    part = ref.at[pl.ds(0, count)]
    pltpu.make_async_copy(part, part, sem).wait()


def forecast_kernel(
    groups,
    feats,
    state_ref,
    cond_ref,
    pair_ref,
    quad_ref,
    linear_ref,
    forcing_ref,
    out_ref,
    first_hot,
    second_hot,
    tail_index,
    tail_rows,
    square,
    gathered,
    partials,
    arrived,
    fin,
    ag_send,
    ag_recv,
    rs_send,
    rs_recv,
    z_send,
    z_recv,
    p_send,
    p_recv,
    c_send,
    c_recv,
):
    g = lax.axis_index("grp")
    f = lax.axis_index("feat")
    core = lax.rem(f, 2)
    partner = f + 1 - 2 * core
    owned, width = state_ref.shape
    members = owned * feats
    pairs = pair_ref.shape[1]
    whole = pairs // TILE
    rest = pairs - whole * TILE
    own_inputs = linear_ref.shape[0]
    tail = tail_rows.shape[0]

    def plane_peer(r):
        return lax.rem(f + r, feats)

    barrier = pltpu.get_barrier_semaphore()

    @pl.loop(1, feats)
    def _(r):
        pl.semaphore_signal(barrier, inc=1, device_id=(g, plane_peer(r)), device_id_type=MESH)

    @pl.loop(1, groups)
    def _(d):
        pl.semaphore_signal(
            barrier, inc=1, device_id=(lax.rem(g + d, groups), f), device_id_type=MESH
        )

    state = state_ref[...]
    own_forcing = jnp.concatenate(
        [forcing_ref[pl.ds(cond_ref[k], 1), :] for k in range(owned)], axis=0
    )

    lane = lax.broadcasted_iota(jnp.int32, (1, tail), 1)
    own_input = jnp.where(
        (lane >= LINEAR_AT) & (lane < LINEAR_AT + own_inputs),
        f * own_inputs + lane - LINEAR_AT,
        -1,
    )
    tail_index[0:1, :] = own_input
    tail_index[1:2, :] = jnp.full((1, tail), -1, jnp.int32)
    tail_index[:, 0:rest] = pair_ref[:, whole * TILE : pairs]
    tail_rows[...] = jnp.zeros_like(tail_rows)
    tail_rows[0:rest, :] = quad_ref[whole * TILE : pairs, :]
    tail_rows[LINEAR_AT : LINEAR_AT + own_inputs, :] = linear_ref[...]
    tail_ones = jnp.where(own_input >= 0, 1.0, 0.0)

    for table, hot in ((0, first_hot), (1, second_hot)):
        for c in range(whole):
            number = lax.broadcasted_iota(jnp.int32, (width, TILE), 0)
            index = pair_ref[table : table + 1, c * TILE : (c + 1) * TILE]
            hot[:, c * TILE : (c + 1) * TILE] = jnp.where(number == index, 1.0, 0.0).astype(
                jnp.bfloat16
            )
        number = lax.broadcasted_iota(jnp.int32, (width, tail), 0)
        index = tail_index[table : table + 1, :]
        hot[:, whole * TILE : whole * TILE + tail] = jnp.where(number == index, 1.0, 0.0).astype(
            jnp.bfloat16
        )

    gathered[0, f] = state.astype(jnp.bfloat16)
    pl.semaphore_wait(barrier, feats - 1 + groups - 1)

    for step in range(STEPS):
        if step > 0:
            gathered[step, f] = state.astype(jnp.bfloat16)

        @pl.loop(1, feats)
        def _(r):
            pltpu.make_async_remote_copy(
                src_ref=gathered.at[step, f],
                dst_ref=gathered.at[step, f],
                send_sem=ag_send.at[step],
                recv_sem=ag_recv.at[step],
                device_id=(g, plane_peer(r)),
                device_id_type=MESH,
            ).start()

        wait_bytes(gathered.at[step], feats - 1, ag_recv.at[step])
        for r in range(feats):
            square[r * owned : (r + 1) * owned, :] = gathered[step, r].astype(jnp.float32)
        current = square[...].astype(jnp.bfloat16)

        def product(start, size, extra):
            first = jnp.dot(
                current, first_hot[:, start : start + size], preferred_element_type=jnp.float32
            )
            second = jnp.dot(
                current, second_hot[:, start : start + size], preferred_element_type=jnp.float32
            )
            if extra is not None:
                second = second + extra
            return (first * second).astype(jnp.bfloat16)

        total = jnp.dot(
            product(whole * TILE, tail, tail_ones),
            tail_rows[...],
            preferred_element_type=jnp.float32,
        )
        for c in range(whole):
            total = total + jnp.dot(
                product(c * TILE, TILE, None),
                quad_ref[c * TILE : (c + 1) * TILE, :],
                preferred_element_type=jnp.float32,
            )
        square[...] = total
        for r in range(feats):
            partials[step, r] = square[r * owned : (r + 1) * owned, :].astype(jnp.bfloat16)
        arrived[step, f] = partials[step, f]

        @pl.loop(1, feats)
        def _(r):
            peer = plane_peer(r)
            pltpu.make_async_remote_copy(
                src_ref=partials.at[step, peer],
                dst_ref=arrived.at[step, f],
                send_sem=rs_send.at[step],
                recv_sem=rs_recv.at[step],
                device_id=(g, peer),
                device_id_type=MESH,
            ).start()

        wait_bytes(arrived.at[step], feats - 1, rs_recv.at[step])
        summed = jnp.sum(arrived[step].astype(jnp.float32), axis=0)
        state = state + time_step * (summed + own_forcing)

    mine = g * feats + f
    fin[mine] = state.astype(jnp.bfloat16)

    @pl.loop(1, groups)
    def _(d):
        there = lax.rem(g + d, groups)
        pltpu.make_async_remote_copy(
            src_ref=fin.at[mine],
            dst_ref=fin.at[mine],
            send_sem=z_send,
            recv_sem=z_recv.at[g],
            device_id=(there, f),
            device_id_type=MESH,
        ).start()

    half = groups // 2
    order = [(0, (0,))] + [(d, (d, groups - d) if d != half else (d,)) for d in range(1, half + 1)]
    batches = []
    for first in range(0, len(order), 2):
        batches.append([s for _, shifts in order[first : first + 2] for s in shifts])

    def to_plane(number, batch):
        for shift in batch:
            z = lax.rem(g + shift, groups)
            chunk = z * feats + f
            if shift:
                pltpu.make_async_copy(fin.at[chunk], fin.at[chunk], z_recv.at[z]).wait()

            @pl.loop(1, feats // 2)
            def _(k):
                pltpu.make_async_remote_copy(
                    src_ref=fin.at[chunk],
                    dst_ref=fin.at[chunk],
                    send_sem=p_send,
                    recv_sem=p_recv.at[number],
                    device_id=(g, plane_peer(2 * k)),
                    device_id_type=MESH,
                ).start()

    def across(number, batch):
        wait_bytes(fin, (feats // 2 - 1) * len(batch), p_recv.at[number])
        for shift in batch:
            z = lax.rem(g + shift, groups)

            @pl.loop(0, feats // 2)
            def _(k):
                chunk = z * feats + 2 * k + core
                pltpu.make_async_remote_copy(
                    src_ref=fin.at[chunk],
                    dst_ref=fin.at[chunk],
                    send_sem=c_send,
                    recv_sem=c_recv.at[number],
                    device_id=(g, partner),
                    device_id_type=MESH,
                ).start()

    def settle(number, batch):
        wait_bytes(fin, feats // 2 * len(batch), c_recv.at[number])
        for shift in batch:
            z = lax.rem(g + shift, groups)
            for r in range(feats):
                square[r * owned : (r + 1) * owned, :] = fin[z * feats + r].astype(jnp.float32)
            out_ref[pl.ds(pl.multiple_of(z * members, members), members), :] = square[...].astype(
                jnp.bfloat16
            )

    count = len(batches)
    for number in range(count + 2):
        if number < count:
            to_plane(number, batches[number])
        if 1 <= number <= count:
            across(number - 1, batches[number - 1])
        if number >= 2:
            settle(number - 2, batches[number - 2])

    for step in range(STEPS):
        wait_bytes(gathered.at[step], feats - 1, ag_send.at[step])
        wait_bytes(partials.at[step], feats - 1, rs_send.at[step])
    wait_bytes(fin, groups - 1, z_send)
    wait_bytes(fin, (feats // 2 - 1) * groups, p_send)
    wait_bytes(fin, feats // 2 * groups, c_send)


def forecast(mesh, state, cond, pair_table, quadratic, linear, forcing):
    groups, feats = mesh.shape["grp"], mesh.shape["feat"]
    owned, width = state.shape
    pairs = pair_table.shape[1]
    whole = pairs // TILE
    tail = 128
    assert pairs - whole * TILE <= LINEAR_AT and LINEAR_AT + linear.shape[0] <= tail
    batches = (groups // 2 + 2) // 2
    vmem = pl.BlockSpec(memory_space=pltpu.VMEM)
    bf16 = jnp.bfloat16
    dma = pltpu.SemaphoreType.DMA
    return pl.pallas_call(
        functools.partial(forecast_kernel, groups, feats),
        name="forecast",
        out_shape=jax.ShapeDtypeStruct((groups * feats * owned, width), bf16),
        in_specs=[vmem, pl.BlockSpec(memory_space=pltpu.SMEM), vmem, vmem, vmem, vmem],
        out_specs=vmem,
        scratch_shapes=[
            pltpu.VMEM((width, whole * TILE + tail), bf16),
            pltpu.VMEM((width, whole * TILE + tail), bf16),
            pltpu.VMEM((2, tail), jnp.int32),
            pltpu.VMEM((tail, width), bf16),
            pltpu.VMEM((feats * owned, width), jnp.float32),
            pltpu.VMEM((STEPS, feats, owned, width), bf16),
            pltpu.VMEM((STEPS, feats, owned, width), bf16),
            pltpu.VMEM((STEPS, feats, owned, width), bf16),
            pltpu.VMEM((groups * feats, owned, width), bf16),
            dma((STEPS,)),
            dma((STEPS,)),
            dma((STEPS,)),
            dma((STEPS,)),
            dma,
            dma((groups,)),
            dma,
            dma((batches,)),
            dma,
            dma((batches,)),
        ],
        compiler_params=pltpu.CompilerParams(collective_id=0, has_side_effects=True),
    )(state, cond, pair_table, quadratic, linear, forcing)


def lift_kernel(fin_ref, basis_ref, mean_ref, weight_ref, heat_ref, means):
    cells = basis_ref.shape[1]

    @pl.when(pl.program_id(0) == 0)
    def _():
        for v in range(2):
            row = jnp.broadcast_to(mean_ref[v : v + 1, :], (128, cells))
            means[v] = row.T

    def field(v):
        product = lax.dot_general(
            basis_ref[v],
            fin_ref[...],
            (((1,), (1,)), ((), ())),
            preferred_element_type=jnp.float32,
        )
        columns = [
            product[:, at : at + 128] + means[v] for at in range(0, product.shape[1], 128)
        ]
        return jnp.concatenate(columns, axis=1)

    volume = jnp.maximum(field(0), min_volume)
    weight_ref[...] = (1.0 / volume).astype(jnp.bfloat16)
    heat_ref[...] = (field(1) * volume).astype(jnp.bfloat16)


def lift_back_solution(final, basis, mean_fields):
    members, width = final.shape
    cells = basis.shape[1]
    tile = 256
    out = jax.ShapeDtypeStruct((cells, members), jnp.bfloat16)
    block = pl.BlockSpec((cells, tile), lambda i: (0, i))
    return pl.pallas_call(
        lift_kernel,
        name="lift",
        grid=(members // tile,),
        in_specs=[
            pl.BlockSpec((tile, width), lambda i: (i, 0)),
            pl.BlockSpec((2, cells, width), lambda i: (0, 0, 0)),
            pl.BlockSpec((2, cells), lambda i: (0, 0)),
        ],
        out_specs=[block, block],
        out_shape=[out, out],
        scratch_shapes=[pltpu.VMEM((2, cells, 128), jnp.float32)],
    )(final, basis, mean_fields)


def solution(mesh):
    def per_device(state, cond, pair_table, quadratic, linear, forcing, basis, mean_fields):
        final = forecast(mesh, state, cond, pair_table, quadratic, linear, forcing)
        weight, heat = lift_back_solution(final, basis, mean_fields)
        return (weight, heat)

    return jax.shard_map(
        per_device,
        mesh=mesh,
        in_specs=(
            P(("grp", "feat"), None),
            P(("grp", "feat")),
            P(None, "feat"),
            P("feat", None),
            P("feat", None),
            P(),
            P(None, ("grp", "feat"), None),
            P(None, ("grp", "feat")),
        ),
        out_specs=(P(("grp", "feat"), None), P(("grp", "feat"), None)),
        check_vma=False,
    )
```

time: 563 us -> 74.5 us (0.13)
  waiting for transfers between devices: 455 us -> 0 us
  Pallas kernels: 0 us -> 73.6 us
  blocking collectives: 53.7 us -> 0 us
  local copies, waits for them, and re-layouts: 24.9 us -> 0 us
  between operations: 14.6 us -> 0.64 us
  matrix products: 9.81 us -> 0 us
    unnamed x5 -> x0, waiting for transfers between devices: 257 us -> none
    all_gather x1 -> x0, waiting for transfers between devices: 198 us -> none  [per_device(): lax.all_gather(latent_vectors.astype(jnp.bfloat16), ('grp', 'feat'), axis...]
    pallas_call x0 -> x2, Pallas kernels: none -> 73.6 us  [the longest x1 66.1 us: forecast(): pl.pallas_call(functools.partial(forecast_kernel, groups, feats), name='f...]
    all_gather x2 -> x0, blocking collectives: 53.7 us -> none  [the longest x1 29.1 us: per_device(): lax.all_gather(starting_latent_vectors, 'feat', axis=0, tiled=True)]
    gather x4 -> x0, local copies, waits for them, and re-layouts: 19.5 us -> none  [the longest x2 11.2 us: drift_terms(): jnp.take(latent_vectors, first_index, axis=1)]
    dot_general x6 -> x0, matrix products: 9.81 us -> none  [the longest x2 6.51 us: drift_terms(): jnp.dot(features, quadratic, preferred_element_type=jnp.float32)]
  transfers between devices with their start and end apart: 3 -> 0, of which waited for: 3 -> 0; matrix products, arithmetic and copies ran while one was open for 0% -> 0% of each run, Pallas kernels for 0% -> 0%
where the time goes in v1:
time: 74.5 us; the launch traced here: 74.2 us
  Pallas kernels  73.6 us (99%)
    pallas_call x1, Pallas kernels, forecast(): pl.pallas_call(functools.partial(forecast_kernel, groups, feats), name='f...  66.1 us
    pallas_call x1, Pallas kernels, lift_back_solution(): pl.pallas_call(lift_kernel, name='lift', grid=(members // tile,), in_spec...  7.43 us

profile of v1, /device:TPU:1, one launch (start us, length us, event | category | flops | bytes accessed | tf_op | source)
XLA Modules:
  0.0 74.2 jit_solution(5999502692367799538)
XLA Ops:
  0.6 66.1 %forecast.1.fin_ref = bf16[2048,384]{1,0:T(8,128)(2,1)} custom-call(f32[4,384]{1,0:T(4,128)} %state_ref.1, s32[4]{0:T(128)} %cond_ref.1, s32[2,2310]{1,0:T(2,128)} %pair_ref.1, bf16[2310,384]{1,0:T(8,128)(2,1)} %quad_ref.1, bf16[12,384]{1,0:T(8,128)(2,1)} %linear_ref.1, f32[8,384]{1,0:T(8,128)} %forcing_ref.1), custom_call_target="tpu_custom_call" | custom-call | tf_op jit(solution)/shard_map/forecast/pallas_call | solution.py:272
  66.8 7.4 %lift.1 = (bf16[336,2048]{1,0:T(8,128)(2,1)}, bf16[336,2048]{1,0:T(8,128)(2,1)}) custom-call(bf16[2048,384]{1,0:T(8,128)(2,1)} %forecast.1.fin_ref, bf16[2,336,384]{2,1,0:T(8,128)(2,1)} %basis_ref.1, f32[2,336]{1,0:T(2,128)} %mean_ref.1), custom_call_target="tpu_custom_call" | custom-call | tf_op jit(solution)/shard_map/lift/pallas_call | solution.py:335

commit v2 on v1

v2 whole, which is shorter than its diff:
```python
import functools

import jax
import jax.numpy as jnp
from jax import lax
from jax.experimental import pallas as pl
from jax.experimental.pallas import tpu as pltpu
from jax.sharding import PartitionSpec as P

STEPS = 2
time_step = 0.25
min_volume = 0.25
MESH = pl.DeviceIdType.MESH
TILE = 256
LINEAR_AT = 16
SIDE = 4


def wait_bytes(ref, count, sem):
    part = ref.at[pl.ds(0, count)]
    pltpu.make_async_copy(part, part, sem).wait()


def forecast_kernel(
    groups,
    feats,
    state_hbm,
    cond_hbm,
    pair_hbm,
    quad_hbm,
    linear_hbm,
    forcing_hbm,
    out_hbm,
    state_ref,
    cond_ref,
    pair_ref,
    quad_ref,
    linear_ref,
    forcing_ref,
    first_hot,
    second_hot,
    tail_index,
    tail_rows,
    gathered,
    partials,
    arrived,
    fin,
    rows,
    load_sem,
    ag_send,
    ag_recv,
    rs_send,
    rs_recv,
    z_send,
    z_recv,
    plane_send,
    plane_recv,
    cross_send,
    cross_recv,
    store_sem,
):
    g = lax.axis_index("grp")
    f = lax.axis_index("feat")
    core = lax.rem(f, 2)
    at_x = lax.rem(f // 2, SIDE)
    at_y = f // (2 * SIDE)
    owned, width = state_ref.shape
    members = owned * feats
    pairs = pair_ref.shape[1]
    whole = pairs // TILE
    rest = pairs - whole * TILE
    own_inputs = linear_ref.shape[0]
    tail = tail_rows.shape[0]
    half = groups // 2

    def plane_peer(r):
        return lax.rem(f + r, feats)

    barrier = pltpu.get_barrier_semaphore()

    @pl.loop(1, groups)
    def _(d):
        pl.semaphore_signal(
            barrier, inc=1, device_id=(lax.rem(g + d, groups), f), device_id_type=MESH
        )

    @pl.loop(1, feats)
    def _(r):
        pl.semaphore_signal(barrier, inc=1, device_id=(g, plane_peer(r)), device_id_type=MESH)

    loads = [
        pltpu.make_async_copy(source, target, load_sem.at[k])
        for k, (source, target) in enumerate(
            (
                (state_hbm, state_ref),
                (cond_hbm, cond_ref),
                (forcing_hbm, forcing_ref),
                (pair_hbm, pair_ref),
                (linear_hbm, linear_ref),
                (quad_hbm, quad_ref),
            )
        )
    ]
    for load in loads:
        load.start()
    for load in loads[:3]:
        load.wait()
    state = state_ref[...]
    own_forcing = jnp.concatenate(
        [forcing_ref[pl.ds(cond_ref[k], 1), :] for k in range(owned)], axis=0
    )
    gathered[0, f] = state.astype(jnp.bfloat16)
    pl.semaphore_wait(barrier, feats - 1 + groups - 1)

    def gather_states(step):
        @pl.loop(1, feats)
        def _(r):
            pltpu.make_async_remote_copy(
                src_ref=gathered.at[step, f],
                dst_ref=gathered.at[step, f],
                send_sem=ag_send.at[step],
                recv_sem=ag_recv.at[step],
                device_id=(g, plane_peer(r)),
                device_id_type=MESH,
            ).start()

    gather_states(0)
    for load in loads[3:]:
        load.wait()
    lane = lax.broadcasted_iota(jnp.int32, (1, tail), 1)
    own_input = jnp.where(
        (lane >= LINEAR_AT) & (lane < LINEAR_AT + own_inputs),
        f * own_inputs + lane - LINEAR_AT,
        -1,
    )
    tail_index[0:1, :] = own_input
    tail_index[1:2, :] = jnp.full((1, tail), -1, jnp.int32)
    tail_index[:, 0:rest] = pair_ref[:, whole * TILE : pairs]
    tail_rows[...] = jnp.zeros_like(tail_rows)
    tail_rows[0:rest, :] = quad_ref[whole * TILE : pairs, :]
    tail_rows[LINEAR_AT : LINEAR_AT + own_inputs, :] = linear_ref[...]
    tail_ones = jnp.where(own_input >= 0, 1.0, 0.0)

    for table, hot in ((0, first_hot), (1, second_hot)):
        for c in range(whole):
            number = lax.broadcasted_iota(jnp.int32, (width, TILE), 0)
            index = pair_ref[table : table + 1, c * TILE : (c + 1) * TILE]
            hot[:, c * TILE : (c + 1) * TILE] = jnp.where(number == index, 1.0, 0.0).astype(
                jnp.bfloat16
            )
        number = lax.broadcasted_iota(jnp.int32, (width, tail), 0)
        index = tail_index[table : table + 1, :]
        hot[:, whole * TILE : whole * TILE + tail] = jnp.where(number == index, 1.0, 0.0).astype(
            jnp.bfloat16
        )

    for step in range(STEPS):
        if step > 0:
            gathered[step, f] = state.astype(jnp.bfloat16)
            gather_states(step)

        wait_bytes(gathered.at[step], feats - 1, ag_recv.at[step])
        current = gathered[step].reshape(members, width)

        def product(start, size, extra):
            first = jnp.dot(
                current, first_hot[:, start : start + size], preferred_element_type=jnp.float32
            )
            second = jnp.dot(
                current, second_hot[:, start : start + size], preferred_element_type=jnp.float32
            )
            if extra is not None:
                second = second + extra
            return (first * second).astype(jnp.bfloat16)

        total = jnp.dot(
            product(whole * TILE, tail, tail_ones),
            tail_rows[...],
            preferred_element_type=jnp.float32,
        )
        for c in range(whole):
            total = total + jnp.dot(
                product(c * TILE, TILE, None),
                quad_ref[c * TILE : (c + 1) * TILE, :],
                preferred_element_type=jnp.float32,
            )
        partials[step] = total.astype(jnp.bfloat16).reshape(feats, owned, width)
        arrived[step, f] = partials[step, f]

        @pl.loop(1, feats)
        def _(r):
            peer = plane_peer(r)
            pltpu.make_async_remote_copy(
                src_ref=partials.at[step, peer],
                dst_ref=arrived.at[step, f],
                send_sem=rs_send.at[step],
                recv_sem=rs_recv.at[step],
                device_id=(g, peer),
                device_id_type=MESH,
            ).start()

        wait_bytes(arrived.at[step], feats - 1, rs_recv.at[step])
        summed = jnp.sum(arrived[step].astype(jnp.float32), axis=0)
        state = state + time_step * (summed + own_forcing)

    fin[half, at_y, at_x, core] = state.astype(jnp.bfloat16)

    @pl.loop(1, groups)
    def _(k):
        d = lax.rem(half + groups + (1 - 2 * lax.rem(k, 2)) * (k // 2), groups)
        position = lax.rem(groups + half - d, groups)
        pltpu.make_async_remote_copy(
            src_ref=fin.at[half, at_y, at_x, core],
            dst_ref=fin.at[position, at_y, at_x, core],
            send_sem=z_send,
            recv_sem=z_recv.at[position],
            device_id=(lax.rem(g + d, groups), f),
            device_id_type=MESH,
        ).start()

    plane_copies = {}
    cross_copies = {}
    stores = []

    def to_plane(number, path, stage):
        start, size = batches[number][path]
        span = pl.ds(start, size)
        along_x = stage == path
        if stage == 0:
            view = fin.at[span, at_y, at_x, core]
        elif along_x:
            view = fin.at[span, :, at_x, core]
        else:
            view = fin.at[span, at_y, :, core]
        for k, by in enumerate((2, 1, 3)):
            y, x = at_y, at_x
            if along_x:
                x = lax.rem(at_x + by, SIDE)
            else:
                y = lax.rem(at_y + by, SIDE)
            copy = pltpu.make_async_remote_copy(
                src_ref=view,
                dst_ref=view,
                send_sem=plane_send.at[number, path, stage, k],
                recv_sem=plane_recv.at[number, path, stage, k],
                device_id=(g, (y * SIDE + x) * 2 + core),
                device_id_type=MESH,
            )
            plane_copies[number, path, stage, k] = copy
            copy.start()

    def first_stage(number):
        for path in range(2):
            start, size = batches[number][path]
            for position in range(start, start + size):
                if position != half:
                    spot = fin.at[position, at_y, at_x, core]
                    pltpu.make_async_copy(spot, spot, z_recv.at[position]).wait()
            to_plane(number, path, 0)

    def second_stage(number):
        for path in range(2):
            for k in range(3):
                plane_copies[number, path, 0, k].wait_recv()
            to_plane(number, path, 1)

    def across(number):
        for path in range(2):
            for k in range(3):
                plane_copies[number, path, 1, k].wait_recv()
            start, size = batches[number][path]
            view = fin.at[pl.ds(start, size), :, :, core]
            copy = pltpu.make_async_remote_copy(
                src_ref=view,
                dst_ref=view,
                send_sem=cross_send.at[number, path],
                recv_sem=cross_recv.at[number, path],
                device_id=(g, f + 1 - 2 * core),
                device_id_type=MESH,
            )
            cross_copies[number, path] = copy
            copy.start()

    def settle(number):
        for path in range(2):
            cross_copies[number, path].wait_recv()
            start, size = batches[number][path]
            for position in range(start, start + size):
                z = lax.rem(g + position + half, groups)
                rows[position] = fin[position].reshape(members, width)
                store = pltpu.make_async_copy(
                    rows.at[position],
                    out_hbm.at[pl.ds(pl.multiple_of(z * members, members), members)],
                    store_sem.at[position],
                )
                store.start()
                stores.append(store)

    quarter = half // 2
    batches = (
        ((half, quarter), (half - quarter, quarter)),
        ((half + quarter, half - quarter), (0, half - quarter)),
    )
    first_stage(0)
    second_stage(0)
    first_stage(1)
    second_stage(1)
    across(0)
    settle(0)
    across(1)
    settle(1)

    for step in range(STEPS):
        wait_bytes(gathered.at[step], feats - 1, ag_send.at[step])
        wait_bytes(partials.at[step], feats - 1, rs_send.at[step])
    sent = fin.at[pl.ds(0, groups - 1), 0, 0, 0]
    pltpu.make_async_copy(sent, sent, z_send).wait()
    for copy in (*plane_copies.values(), *cross_copies.values()):
        copy.wait_send()
    for store in stores:
        store.wait()


def forecast(mesh, state, cond, pair_table, quadratic, linear, forcing):
    groups, feats = mesh.shape["grp"], mesh.shape["feat"]
    owned, width = state.shape
    pairs = pair_table.shape[1]
    whole = pairs // TILE
    tail = 128
    assert pairs - whole * TILE <= LINEAR_AT and LINEAR_AT + linear.shape[0] <= tail
    assert feats == 2 * SIDE * SIDE and groups % 4 == 0
    anywhere = pl.BlockSpec(memory_space=pl.ANY)
    bf16 = jnp.bfloat16
    dma = pltpu.SemaphoreType.DMA
    return pl.pallas_call(
        functools.partial(forecast_kernel, groups, feats),
        name="forecast",
        out_shape=jax.ShapeDtypeStruct((groups * feats * owned, width), bf16),
        in_specs=[anywhere] * 6,
        out_specs=anywhere,
        scratch_shapes=[
            pltpu.VMEM(state.shape, state.dtype),
            pltpu.SMEM(cond.shape, cond.dtype),
            pltpu.VMEM(pair_table.shape, pair_table.dtype),
            pltpu.VMEM(quadratic.shape, quadratic.dtype),
            pltpu.VMEM(linear.shape, linear.dtype),
            pltpu.VMEM(forcing.shape, forcing.dtype),
            pltpu.VMEM((width, whole * TILE + tail), bf16),
            pltpu.VMEM((width, whole * TILE + tail), bf16),
            pltpu.VMEM((2, tail), jnp.int32),
            pltpu.VMEM((tail, width), bf16),
            pltpu.VMEM((STEPS, feats, owned, width), bf16),
            pltpu.VMEM((STEPS, feats, owned, width), bf16),
            pltpu.VMEM((STEPS, feats, owned, width), bf16),
            pltpu.VMEM((groups, SIDE, SIDE, 2, owned, width), bf16),
            pltpu.VMEM((groups, feats * owned, width), bf16),
            dma((6,)),
            dma((STEPS,)),
            dma((STEPS,)),
            dma((STEPS,)),
            dma((STEPS,)),
            dma,
            dma((groups,)),
            dma((2, 2, 2, 3)),
            dma((2, 2, 2, 3)),
            dma((2, 2)),
            dma((2, 2)),
            dma((groups,)),
        ],
        compiler_params=pltpu.CompilerParams(collective_id=0, has_side_effects=True),
    )(state, cond, pair_table, quadratic, linear, forcing)


def lift_kernel(fin_ref, basis_ref, mean_ref, weight_ref, heat_ref, means):
    cells = basis_ref.shape[1]

    @pl.when(pl.program_id(0) == 0)
    def _():
        for v in range(2):
            row = jnp.broadcast_to(mean_ref[v : v + 1, :], (128, cells))
            means[v] = row.T

    def field(v):
        product = lax.dot_general(
            basis_ref[v],
            fin_ref[...],
            (((1,), (1,)), ((), ())),
            preferred_element_type=jnp.float32,
        )
        columns = [
            product[:, at : at + 128] + means[v] for at in range(0, product.shape[1], 128)
        ]
        return jnp.concatenate(columns, axis=1)

    volume = jnp.maximum(field(0), min_volume)
    weight_ref[...] = (1.0 / volume).astype(jnp.bfloat16)
    heat_ref[...] = (field(1) * volume).astype(jnp.bfloat16)


def lift_back_solution(final, basis, mean_fields):
    members, width = final.shape
    cells = basis.shape[1]
    tile = 1024
    out = jax.ShapeDtypeStruct((cells, members), jnp.bfloat16)
    block = pl.BlockSpec((cells, tile), lambda i: (0, i))
    return pl.pallas_call(
        lift_kernel,
        name="lift",
        grid=(members // tile,),
        in_specs=[
            pl.BlockSpec((tile, width), lambda i: (i, 0)),
            pl.BlockSpec((2, cells, width), lambda i: (0, 0, 0)),
            pl.BlockSpec((2, cells), lambda i: (0, 0)),
        ],
        out_specs=[block, block],
        out_shape=[out, out],
        scratch_shapes=[pltpu.VMEM((2, cells, 128), jnp.float32)],
    )(final, basis, mean_fields)


def solution(mesh):
    def per_device(state, cond, pair_table, quadratic, linear, forcing, basis, mean_fields):
        final = forecast(mesh, state, cond, pair_table, quadratic, linear, forcing)
        weight, heat = lift_back_solution(final, basis, mean_fields)
        return (weight, heat)

    return jax.shard_map(
        per_device,
        mesh=mesh,
        in_specs=(
            P(("grp", "feat"), None),
            P(("grp", "feat")),
            P(None, "feat"),
            P("feat", None),
            P("feat", None),
            P(),
            P(None, ("grp", "feat"), None),
            P(None, ("grp", "feat")),
        ),
        out_specs=(P(("grp", "feat"), None), P(("grp", "feat"), None)),
        check_vma=False,
    )
```

time: 74.5 us -> 65.9 us (0.88)
  Pallas kernels: 73.6 us -> 65.1 us
    pallas_call x1, Pallas kernels: 66.1 us -> 60.9 us  [forecast(): pl.pallas_call(functools.partial(forecast_kernel, groups, feats), name='f...]
    pallas_call x1, Pallas kernels: 7.43 us -> 4.17 us  [lift_back_solution(): pl.pallas_call(lift_kernel, name='lift', grid=(members // tile,), in_spec...]
where the time goes in v2:
time: 65.9 us; the launch traced here: 65.7 us
  Pallas kernels  65.1 us (99%)
    pallas_call x1, Pallas kernels, forecast(): pl.pallas_call(functools.partial(forecast_kernel, groups, feats), name='f...  60.9 us
    pallas_call x1, Pallas kernels, lift_back_solution(): pl.pallas_call(lift_kernel, name='lift', grid=(members // tile,), in_spec...  4.17 us

profile of v2, /device:TPU:1, one launch (start us, length us, event | category | flops | bytes accessed | tf_op | source)
XLA Modules:
  0.0 65.7 jit_solution(3946987551440423143)
XLA Ops:
  0.6 60.9 %forecast.1.fin_ref = bf16[2048,384]{1,0:T(8,128)(2,1)} custom-call(f32[4,384]{1,0:T(4,128)} %state_hbm.1, s32[4]{0:T(128)} %cond_hbm.1, s32[2,2310]{1,0:T(2,128)} %pair_hbm.1, bf16[2310,384]{1,0:T(8,128)(2,1)} %quad_hbm.1, bf16[12,384]{1,0:T(8,128)(2,1)} %linear_hbm.1, f32[8,384]{1,0:T(8,128)} %forcing_hbm.1), custom_call_target="tpu_custom_call" | custom-call | tf_op jit(solution)/shard_map/forecast/pallas_call | solution.py:335
  61.5 4.2 %lift.1 = (bf16[336,2048]{1,0:T(8,128)(2,1)}, bf16[336,2048]{1,0:T(8,128)(2,1)}) custom-call(bf16[2048,384]{1,0:T(8,128)(2,1)} %forecast.1.fin_ref, bf16[2,336,384]{2,1,0:T(8,128)(2,1)} %basis_ref.1, f32[2,336]{1,0:T(2,128)} %mean_ref.1), custom_call_target="tpu_custom_call" | custom-call | tf_op jit(solution)/shard_map/lift/pallas_call | solution.py:406

commit v3 on v2

v3 whole, which is shorter than its diff:
```python
import functools

import jax
import jax.numpy as jnp
from jax import lax
from jax.experimental import pallas as pl
from jax.experimental.pallas import tpu as pltpu
from jax.sharding import PartitionSpec as P

STEPS = 2
time_step = 0.25
min_volume = 0.25
MESH = pl.DeviceIdType.MESH
TILE = 256
LINEAR_AT = 16
SIDE = 4
SPANS = ((4, 8), (12, 4), (0, 4))


def wait_bytes(ref, count, sem):
    part = ref.at[pl.ds(0, count)]
    pltpu.make_async_copy(part, part, sem).wait()


def forecast_kernel(
    groups,
    feats,
    state_hbm,
    cond_hbm,
    pair_hbm,
    quad_hbm,
    linear_hbm,
    forcing_hbm,
    basis_hbm,
    mean_hbm,
    weight_ref,
    heat_ref,
    state_ref,
    cond_ref,
    pair_ref,
    quad_ref,
    linear_ref,
    forcing_ref,
    first_hot,
    second_hot,
    tail_index,
    tail_rows,
    gathered,
    partials,
    arrived,
    fin,
    basis_ref,
    mean_ref,
    means,
    load_sem,
    ag_send,
    ag_recv,
    rs_send,
    rs_recv,
    z_send,
    z_recv,
    plane_send,
    plane_recv,
    cross_send,
    cross_recv,
):
    g = lax.axis_index("grp")
    f = lax.axis_index("feat")
    core = lax.rem(f, 2)
    at_x = lax.rem(f // 2, SIDE)
    at_y = f // (2 * SIDE)
    owned, width = state_ref.shape
    members = owned * feats
    pairs = pair_ref.shape[1]
    whole = pairs // TILE
    rest = pairs - whole * TILE
    own_inputs = linear_ref.shape[0]
    tail = tail_rows.shape[0]
    half = groups // 2

    def plane_peer(r):
        return lax.rem(f + r, feats)

    def far_peers(cores=True):
        shifts = [
            (y, x, c) for y in range(SIDE) for x in range(SIDE) for c in range(1 + cores)
        ]
        shifts.sort(key=lambda s: -(min(s[0], SIDE - s[0]) + min(s[1], SIDE - s[1])))
        for y, x, c in (t for t in shifts if any(t)):
            to_y, to_x = lax.rem(at_y + y, SIDE), lax.rem(at_x + x, SIDE)
            yield (to_y * SIDE + to_x) * 2 + (1 - core if c else core)

    barrier = pltpu.get_barrier_semaphore()

    @pl.loop(1, groups)
    def _(d):
        pl.semaphore_signal(
            barrier, inc=1, device_id=(lax.rem(g + d, groups), f), device_id_type=MESH
        )

    @pl.loop(1, feats)
    def _(r):
        pl.semaphore_signal(barrier, inc=1, device_id=(g, plane_peer(r)), device_id_type=MESH)

    loads = [
        pltpu.make_async_copy(source, target, load_sem.at[k])
        for k, (source, target) in enumerate(
            (
                (state_hbm, state_ref),
                (cond_hbm, cond_ref),
                (forcing_hbm, forcing_ref),
                (pair_hbm, pair_ref),
                (linear_hbm, linear_ref),
                (quad_hbm, quad_ref),
                (basis_hbm, basis_ref),
                (mean_hbm, mean_ref),
            )
        )
    ]
    for load in loads:
        load.start()
    for load in loads[:3]:
        load.wait()
    state = state_ref[...]
    own_forcing = jnp.concatenate(
        [forcing_ref[pl.ds(cond_ref[k], 1), :] for k in range(owned)], axis=0
    )
    gathered[0, f] = state.astype(jnp.bfloat16)
    pl.semaphore_wait(barrier, feats - 1 + groups - 1)

    def gather_states(step):
        for peer in far_peers():
            pltpu.make_async_remote_copy(
                src_ref=gathered.at[step, f],
                dst_ref=gathered.at[step, f],
                send_sem=ag_send.at[step],
                recv_sem=ag_recv.at[step],
                device_id=(g, peer),
                device_id_type=MESH,
            ).start()

    gather_states(0)
    for load in loads[3:6]:
        load.wait()
    lane = lax.broadcasted_iota(jnp.int32, (1, tail), 1)
    own_input = jnp.where(
        (lane >= LINEAR_AT) & (lane < LINEAR_AT + own_inputs),
        f * own_inputs + lane - LINEAR_AT,
        -1,
    )
    tail_index[0:1, :] = own_input
    tail_index[1:2, :] = jnp.full((1, tail), -1, jnp.int32)
    tail_index[:, 0:rest] = pair_ref[:, whole * TILE : pairs]
    tail_rows[...] = jnp.zeros_like(tail_rows)
    tail_rows[0:rest, :] = quad_ref[whole * TILE : pairs, :]
    tail_rows[LINEAR_AT : LINEAR_AT + own_inputs, :] = linear_ref[...]
    tail_ones = jnp.where(own_input >= 0, 1.0, 0.0)

    for table, hot in ((0, first_hot), (1, second_hot)):
        for c in range(whole):
            number = lax.broadcasted_iota(jnp.int32, (width, TILE), 0)
            index = pair_ref[table : table + 1, c * TILE : (c + 1) * TILE]
            hot[:, c * TILE : (c + 1) * TILE] = jnp.where(number == index, 1.0, 0.0).astype(
                jnp.bfloat16
            )
        number = lax.broadcasted_iota(jnp.int32, (width, tail), 0)
        index = tail_index[table : table + 1, :]
        hot[:, whole * TILE : whole * TILE + tail] = jnp.where(number == index, 1.0, 0.0).astype(
            jnp.bfloat16
        )

    for step in range(STEPS):
        if step > 0:
            gathered[step, f] = state.astype(jnp.bfloat16)
            gather_states(step)

        wait_bytes(gathered.at[step], feats - 1, ag_recv.at[step])
        current = gathered[step].reshape(members, width)

        def product(start, size, extra):
            first = jnp.dot(
                current, first_hot[:, start : start + size], preferred_element_type=jnp.float32
            )
            second = jnp.dot(
                current, second_hot[:, start : start + size], preferred_element_type=jnp.float32
            )
            if extra is not None:
                second = second + extra
            return (first * second).astype(jnp.bfloat16)

        total = jnp.dot(
            product(whole * TILE, tail, tail_ones),
            tail_rows[...],
            preferred_element_type=jnp.float32,
        )
        for c in range(whole):
            total = total + jnp.dot(
                product(c * TILE, TILE, None),
                quad_ref[c * TILE : (c + 1) * TILE, :],
                preferred_element_type=jnp.float32,
            )
        partials[step] = total.astype(jnp.bfloat16).reshape(feats, owned, width)
        arrived[step, f] = partials[step, f]

        for peer in far_peers():
            pltpu.make_async_remote_copy(
                src_ref=partials.at[step, peer],
                dst_ref=arrived.at[step, f],
                send_sem=rs_send.at[step],
                recv_sem=rs_recv.at[step],
                device_id=(g, peer),
                device_id_type=MESH,
            ).start()

        wait_bytes(arrived.at[step], feats - 1, rs_recv.at[step])
        summed = jnp.sum(arrived[step].astype(jnp.float32), axis=0)
        state = state + time_step * (summed + own_forcing)

    fin[half, at_y, at_x, core] = state.astype(jnp.bfloat16)

    @pl.loop(1, groups)
    def _(k):
        d = lax.rem(groups + (2 * lax.rem(k, 2) - 1) * ((k + 1) // 2), groups)
        position = lax.rem(groups + half - d, groups)
        pltpu.make_async_remote_copy(
            src_ref=fin.at[half, at_y, at_x, core],
            dst_ref=fin.at[position, at_y, at_x, core],
            send_sem=z_send,
            recv_sem=z_recv.at[position],
            device_id=(lax.rem(g + d, groups), f),
            device_id_type=MESH,
        ).start()

    for load in loads[6:]:
        load.wait()
    for v in range(2):
        means[v] = jnp.broadcast_to(mean_ref[v : v + 1, :], (128, mean_ref.shape[1])).T
    sends = []
    cross_copies = {}

    def to_plane(number):
        start, size = spans[number]
        for position in range(start, start + size):
            if position != half:
                spot = fin.at[position, at_y, at_x, core]
                pltpu.make_async_copy(spot, spot, z_recv.at[position]).wait()
        view = fin.at[pl.ds(start, size), at_y, at_x, core]
        for k, peer in enumerate(far_peers(False)):
            copy = pltpu.make_async_remote_copy(
                src_ref=view,
                dst_ref=view,
                send_sem=plane_send.at[number, k],
                recv_sem=plane_recv.at[number],
                device_id=(g, peer),
                device_id_type=MESH,
            )
            copy.start()
            sends.append(copy)

    def across(number):
        start, size = spans[number]
        span = pl.ds(start, size)
        landed = fin.at[pl.ds(0, SIDE * SIDE - 1), :, pl.ds(0, size // SIDE), core]
        pltpu.make_async_copy(landed, landed, plane_recv.at[number]).wait()
        view = fin.at[span, :, :, core]
        copy = pltpu.make_async_remote_copy(
            src_ref=view,
            dst_ref=view,
            send_sem=cross_send.at[number],
            recv_sem=cross_recv.at[number],
            device_id=(g, f + 1 - 2 * core),
            device_id_type=MESH,
        )
        cross_copies[number] = copy
        copy.start()

    def settle(number):
        cross_copies[number].wait_recv()
        start, size = spans[number]
        for position in range(start, start + size, 2):
            final = fin[position : position + 2].reshape(2 * members, width)
            spots = [
                pl.ds(pl.multiple_of(lax.rem(g + p + half, groups) * members, members), members)
                for p in (position, position + 1)
            ]

            def field(v):
                product = lax.dot_general(
                    basis_ref[v], final, (((1,), (1,)), ((), ())), preferred_element_type=jnp.float32
                )
                return [product[:, at : at + members] + means[v] for at in (0, members)]

            for spot, volume, pressure in zip(spots, field(0), field(1)):
                volume = jnp.maximum(volume, min_volume)
                weight_ref[:, spot] = (1.0 / volume).astype(jnp.bfloat16)
                heat_ref[:, spot] = (pressure * volume).astype(jnp.bfloat16)

    spans = SPANS
    for number in range(len(spans)):
        to_plane(number)
    for number in range(len(spans) + 1):
        if number < len(spans):
            across(number)
        if number > 0:
            settle(number - 1)

    for step in range(STEPS):
        wait_bytes(gathered.at[step], feats - 1, ag_send.at[step])
        wait_bytes(partials.at[step], feats - 1, rs_send.at[step])
    sent = fin.at[pl.ds(0, groups - 1), 0, 0, 0]
    pltpu.make_async_copy(sent, sent, z_send).wait()
    for copy in (*sends, *cross_copies.values()):
        copy.wait_send()


def forecast(mesh, state, cond, pair_table, quadratic, linear, forcing, basis, mean_fields):
    groups, feats = mesh.shape["grp"], mesh.shape["feat"]
    owned, width = state.shape
    pairs = pair_table.shape[1]
    whole = pairs // TILE
    tail = 128
    cells = basis.shape[1]
    assert feats * owned == 128
    assert pairs - whole * TILE <= LINEAR_AT and LINEAR_AT + linear.shape[0] <= tail
    assert feats == 2 * SIDE * SIDE and groups == 16
    anywhere = pl.BlockSpec(memory_space=pl.ANY)
    bf16 = jnp.bfloat16
    dma = pltpu.SemaphoreType.DMA
    return pl.pallas_call(
        functools.partial(forecast_kernel, groups, feats),
        name="forecast",
        out_shape=[pltpu.VMEM((cells, groups * feats * owned), bf16)] * 2,
        in_specs=[anywhere] * 8,
        out_specs=[pl.BlockSpec(memory_space=pltpu.VMEM)] * 2,
        scratch_shapes=[
            pltpu.VMEM(state.shape, state.dtype),
            pltpu.SMEM(cond.shape, cond.dtype),
            pltpu.VMEM(pair_table.shape, pair_table.dtype),
            pltpu.VMEM(quadratic.shape, quadratic.dtype),
            pltpu.VMEM(linear.shape, linear.dtype),
            pltpu.VMEM(forcing.shape, forcing.dtype),
            pltpu.VMEM((width, whole * TILE + tail), bf16),
            pltpu.VMEM((width, whole * TILE + tail), bf16),
            pltpu.VMEM((2, tail), jnp.int32),
            pltpu.VMEM((tail, width), bf16),
            pltpu.VMEM((STEPS, feats, owned, width), bf16),
            pltpu.VMEM((STEPS, feats, owned, width), bf16),
            pltpu.VMEM((STEPS, feats, owned, width), bf16),
            pltpu.VMEM((groups, SIDE, SIDE, 2, owned, width), bf16),
            pltpu.VMEM(basis.shape, bf16),
            pltpu.VMEM(mean_fields.shape, jnp.float32),
            pltpu.VMEM((2, cells, 128), jnp.float32),
            dma((8,)),
            dma((STEPS,)),
            dma((STEPS,)),
            dma((STEPS,)),
            dma((STEPS,)),
            dma,
            dma((groups,)),
            dma((len(SPANS), SIDE * SIDE - 1)),
            dma((len(SPANS),)),
            dma((len(SPANS),)),
            dma((len(SPANS),)),
        ],
        compiler_params=pltpu.CompilerParams(collective_id=0, has_side_effects=True),
    )(state, cond, pair_table, quadratic, linear, forcing, basis, mean_fields)


def solution(mesh):
    def per_device(state, cond, pair_table, quadratic, linear, forcing, basis, mean_fields):
        weight, heat = forecast(
            mesh, state, cond, pair_table, quadratic, linear, forcing, basis, mean_fields
        )
        return (weight, heat)

    return jax.shard_map(
        per_device,
        mesh=mesh,
        in_specs=(
            P(("grp", "feat"), None),
            P(("grp", "feat")),
            P(None, "feat"),
            P("feat", None),
            P("feat", None),
            P(),
            P(None, ("grp", "feat"), None),
            P(None, ("grp", "feat")),
        ),
        out_specs=(P(("grp", "feat"), None), P(("grp", "feat"), None)),
        check_vma=False,
    )
```

time: 65.9 us -> 61.4 us (0.932)
  Pallas kernels: 65.1 us -> 58.5 us
  local copies, waits for them, and re-layouts: 0 us -> 2.16 us
    pallas_call x1 -> x0, Pallas kernels: 4.17 us -> none  [lift_back_solution(): pl.pallas_call(lift_kernel, name='lift', grid=(members // tile,), in_spec...]
    pallas_call x1, Pallas kernels: 60.9 us -> 58.5 us  [forecast(): pl.pallas_call(functools.partial(forecast_kernel, groups, feats), name='f...]
    unnamed x0 -> x2, local copies, waits for them, and re-layouts: none -> 2.16 us
where the time goes in v3:
time: 61.4 us; the launch traced here: 61.3 us
  Pallas kernels  58.5 us (95%)
  local copies, waits for them, and re-layouts  2.16 us (4%)
  between operations  0.64 us (1%)
    pallas_call x1, Pallas kernels, forecast(): pl.pallas_call(functools.partial(forecast_kernel, groups, feats), name='f...  58.5 us
    unnamed x2, local copies, waits for them, and re-layouts  2.16 us

profile of v3, /device:TPU:1, one launch (start us, length us, event | category | flops | bytes accessed | tf_op | source)
XLA Modules:
  0.0 61.3 jit_solution(10725957090229851445)
XLA Ops:
  0.6 58.5 %forecast.1 = (bf16[336,2048]{1,0:T(8,128)(2,1)S(1)}, bf16[336,2048]{1,0:T(8,128)(2,1)S(1)}) custom-call(f32[4,384]{1,0:T(4,128)} %state_hbm.1, s32[4]{0:T(128)} %cond_hbm.1, s32[2,2310]{1,0:T(2,128)} %pair_hbm.1, bf16[2310,384]{1,0:T(8,128)(2,1)} %quad_hbm.1, bf16[12,384]{1,0:T(8,128)(2,1)} %linear_hbm.1, f32[8,384]{1,0:T(8,128)} %forcing_hbm.1, ...), custom_call_target="tpu_custom_call" | custom-call | tf_op jit(solution)/shard_map/forecast/pallas_call | solution.py:329
  59.1 1.1 %copy.12 = bf16[336,2048]{1,0:T(8,128)(2,1)} copy(bf16[336,2048]{1,0:T(8,128)(2,1)S(1)} %get-tuple-element.2) | data formatting | bytes 2752512
  60.2 1.1 %copy.13 = bf16[336,2048]{1,0:T(8,128)(2,1)} copy(bf16[336,2048]{1,0:T(8,128)(2,1)S(1)} %get-tuple-element.3) | data formatting | bytes 2752512
